TPU v7x, 32 devices: a whole 2x2x4 slice. The times are simulated.
32 devices in a mesh: field: 2 (over x), expo: 8 (over z, y), sky: 2 (over core).
Axes of the slice: x: 2, y: 2, z: 4, core: 2. Of those that a mesh axis runs over, the one named last changes fastest.
Arguments:
- science: float32 [64, 64, 512], P(('field', 'expo'), 'sky'), parts along dimension 0, may hold values from -6 to 6
- inv_variance: float32 [64, 64, 512], P(('field', 'expo'), 'sky'), parts along dimension 0, may hold values from 0.25 to 4
- pixel_masks: int32 [64, 64, 512], P(('field', 'expo'), 'sky'), parts along dimension 0, may hold values 0 or 1
- point_spread: float32 [64, 5, 5], P(('field', 'expo')), parts along dimension 0, may hold values from 0.02 to 0.1
- tile_offset: int32 [8, 32], P(None, 'expo'), may hold values from 0 to 1
- column_shift: int32 [8, 32], P(None, 'expo'), may hold values from -128 to 128
- trail_kernel: float32 [8, 3, 3], P('expo'), may hold values from 0.1 to 1
Outputs:
- likelihood: float32 [16, 64, 512], P(('field', 'expo'), 'sky'), parts along dimension 0
There are 2 independent parts, one for each index of `field`. A program takes and returns all parts, laid end to end along the dimension named above; an argument that names none is the same for every part. Nothing has to cross between parts.
All inputs are finite; a program needn't handle non-finite values. No bound on the sum of `pixel_masks` on one device may be relied on, other than what follows from the above.
Results may differ from a plain program's by a relative error of at most 0.0003.
Values sent between devices are 32-bit elements; how exact they have to be, the bound alone decides.
A program may use at most 128 MiB of HBM per device.

v0:
```python
import jax
import jax.numpy as jnp
from jax import lax
from jax.sharding import PartitionSpec as P

MAX_SHIFT = 128


def padded_2(block, sides, width):
    for axis, dim in sides:
        count = lax.axis_size(axis)
        forward = [(i, i + 1) for i in range(count - 1)]
        backward = [(target, source) for source, target in forward]
        low = lax.ppermute(
            lax.slice_in_dim(block, block.shape[dim] - width, None, axis=dim), axis, forward
        )
        high = lax.ppermute(lax.slice_in_dim(block, 0, width, axis=dim), axis, backward)
        block = jnp.concatenate([low, block, high], axis=dim)
    return block


def partner(array, axis, bit):
    return lax.ppermute(array, axis, [(i, i ^ 1 << bit) for i in range(lax.axis_size(axis))])


def filter_taps(padded, kernel, row_count, column_count):
    taps = kernel.shape[-1]
    running = jnp.zeros(padded.shape[:-2] + (row_count, column_count), jnp.float32)
    for row_tap in range(taps):
        for column_tap in range(taps):
            running = (
                running
                + kernel[:, row_tap, column_tap, None, None]
                * padded[..., row_tap : row_tap + row_count, column_tap : column_tap + column_count]
            )
    return running


def shift_columns(wide, column_shifts, column_count):
    margin = (wide.shape[-1] - column_count) // 2

    def single(single_image, pixel_shift):
        return lax.dynamic_slice_in_dim(single_image, margin - pixel_shift, column_count, 2)

    return jax.vmap(single, in_axes=(1, 0), out_axes=1)(wide, column_shifts)


def blocked_velocities(velocity_fn, tile_offset, column_shift):
    velocity_count = tile_offset.shape[0]
    exposure_count = tile_offset.shape[1]
    block_size = 4
    block_count = velocity_count // block_size
    offsets = tile_offset.reshape(block_count, block_size, exposure_count)
    shifts = column_shift.reshape(block_count, block_size, exposure_count)

    def one_block(inputs):
        return jax.vmap(velocity_fn)(inputs[0], inputs[1])

    partial_value = lax.map(one_block, (offsets, shifts))
    return partial_value.reshape((velocity_count,) + partial_value.shape[2:])


def shards(
    science, inv_variance, pixel_masks, point_spread, tile_offset, column_shift, trail_kernel
):
    row_count = science.shape[1]
    column_count = science.shape[2]
    margin = MAX_SHIFT
    weighted = inv_variance * pixel_masks.astype(jnp.float32)
    paired = jnp.stack([science * weighted, weighted])
    rimmed = padded_2(paired, (("sky", 2),), 2)
    rimmed = jnp.pad(rimmed, ((0, 0), (0, 0), (0, 0), (2, 2)))
    psi_images = filter_taps(rimmed[0], point_spread, row_count, column_count)
    phi_images = filter_taps(rimmed[1], point_spread * point_spread, row_count, column_count)
    filtered = jnp.stack([psi_images, phi_images])
    padding = ((0, 0), (0, 0), (0, 0), (margin, margin))
    own_wide = jnp.pad(filtered, padding)

    def split_velocity(offsets, column_shifts):
        shifted = shift_columns(own_wide, column_shifts, column_count)
        select_flags = offsets[None, :, None, None] == 1
        near_sum = jnp.sum(jnp.where(select_flags, 0.0, shifted), axis=1)
        far_sum = jnp.sum(jnp.where(select_flags, shifted, 0.0), axis=1)
        return jnp.stack([near_sum, far_sum])

    partial_value = blocked_velocities(split_velocity, tile_offset, column_shift)
    reduced = lax.psum_scatter(partial_value, "expo", scatter_dimension=0, tiled=True)
    arrived = partner(reduced[:, 1], "sky", 0)
    stacks = reduced[:, 0] + arrived
    stack_rimmed = padded_2(stacks, (("sky", 2),), 1)
    stack_rimmed = jnp.pad(stack_rimmed, ((0, 0), (0, 0), (0, 0), (1, 1)))
    psi_trail = filter_taps(stack_rimmed[:, 0], trail_kernel, row_count, column_count)
    phi_trail = filter_taps(
        stack_rimmed[:, 1], trail_kernel * trail_kernel, row_count, column_count
    )
    return psi_trail / jnp.sqrt(phi_trail + 1.0)


def solution(mesh):
    return jax.shard_map(
        shards,
        mesh=mesh,
        in_specs=(
            P(("field", "expo"), "sky", None),
            P(("field", "expo"), "sky", None),
            P(("field", "expo"), "sky", None),
            P(("field", "expo"), None, None),
            P(None, "expo"),
            P(None, "expo"),
            P("expo", None, None),
        ),
        out_specs=P(("field", "expo"), "sky", None),
        check_vma=False,
    )
```

profile of v0, /device:TPU:0, one launch (start us, length us, event | category | flops | bytes accessed | tf_op | source)
XLA Modules:
  0.0 198.7 jit_solution(7919316970326178395)
XLA Ops:
  6.5 1.2 multiply_bitcast_fusion
  7.8 0.3 copy.25
  8.2 2.4 %collective-permute-start = (f32[2,4,2,512]{3,1,2,0:T(4,128)S(1)}, f32[2,4,2,512]{3,1,2,0:T(4,128)S(1)}, u32[]{:S(2)}, u32[]{:S(2)}) collective-permute-start(f32[2,4,2,512]{3,1,2,0:T(4,128)S(1)} %get-tuple-element.150), channel_id=1, source_target_pairs={{0,1},{2,3},{4,5},{6,7},{8,9},{10,11},{12,13},{14,15},{16,17},{18,... | collective-permute-start | bytes 98312 | tf_op jit(solution)/shard_map/ppermute | solution.py:14
  10.6 1.3 collective-permute-start.1
  11.9 0.5 slice_reduce_fusion.49
  12.7 0.5 slice_reduce_fusion.24
  13.7 0.4 select_maximum_fusion
  14.2 2.9 %fusion.31 = f32[1,4,32,512]{3,1,2,0:T(4,128)S(1)} fusion(f32[4,36,516]{2,0,1:T(4,128)S(1)} %get-tuple-element.148, f32[4]{0:T(128)S(1)} %get-tuple-element.112, f32[4]{0:T(128)S(1)} %get-tuple-element.89, f32[4]{0:T(128)S(1)} %get-tuple-element.90, f32[4]{0:T(128)S(1)} %get-tuple-element.91, f32[4]{0:T(128)S(1)} %get-tuple-element.92, ...), kind=kLoop, calls=%fused_computation.74 | loop fusion | flops 3211264 | bytes 6816144 | tf_op jit(solution)/shard_map/stack | solution.py:75
  17.2 2.9 %fusion.6 = f32[1,4,32,512]{3,1,2,0:T(4,128)S(1)} fusion(f32[4,36,516]{2,0,1:T(4,128)S(1)} %get-tuple-element.149, f32[4]{0:T(128)S(1)} %get-tuple-element.114, f32[4]{0:T(128)S(1)} %get-tuple-element.115, f32[4]{0:T(128)S(1)} %get-tuple-element.116, f32[4]{0:T(128)S(1)} %get-tuple-element.117, f32[4]{0:T(128)S(1)} %get-tuple-element.118, ...), kind=kLoop, calls=%fused_computation.24 | loop fusion | flops 3211264 | bytes 6816144 | tf_op jit(solution)/shard_map/stack | solution.py:75
  20.2 1.7 copy.41
  21.9 2.7 %pad.17.clone = f32[2,4,32,768]{2,0,1,3:T(2,128)} pad(f32[2,4,32,512]{2,0,1,3:T(2,128)S(1)} %copy.41, f32[]{:T(128)} %constant.43.clone.1), padding=0_0x0_0x0_0x128_128 | pad | bytes 1310724 | tf_op jit(solution)/shard_map/jit(_pad)/pad | solution.py:77
  24.6 74.5 %while.12 = (s32[]{:T(128)}, f32[2,4,2,2,32,512]{5,4,3,2,1,0:T(8,128)}, s32[2,4,4]{2,1,0:T(4,128)S(1)}, f32[2,4,32,768]{2,0,1,3:T(2,128)}, s32[2,4,4]{2,1,0:T(4,128)S(1)}, /*index=5*/s32[]{:T(128)}) while((s32[]{:T(128)}, f32[2,4,2,2,32,512]{5,4,3,2,1,0:T(8,128)}, s32[2,4,4]{2,1,0:T(4,128)S(1)}, f32[2,4,32,768]{2,0,1,3:T(2,128)}, ...), condition=%wide.region_3.4_spmd, body=%wide.region_0.3_spmd.sunk | while | flops 2097314 | bytes 11535533 | solution.py:59
  24.7 15.0 %gather_fusion = f32[16,2,32,512]{2,1,3,0:T(2,128)} fusion(f32[4,2,32,768]{2,1,0,3:T(2,128)} %bitcast.75, s32[16]{0:T(128)S(1)} %reshape.156), kind=kCustom, calls=%fused_computation.clone.1 | custom fusion | bytes 4194560 | tf_op jit(solution)/shard_map/while/body/eval_jaxpr/vmap(vmap())/gather | solution.py:43
  39.7 17.5 %select_reduce_fusion.3 = (f32[4,2,32,512]{2,1,3,0:T(2,128)S(1)}, f32[4,2,32,512]{2,1,3,0:T(2,128)}) fusion(pred[4,4]{1,0:T(4,128)(4,1)S(1)} %fusion.83, f32[16,2,32,512]{2,1,3,0:T(2,128)} %gather_fusion), kind=kLoop, calls=%fused_computation.2.clone.1 | loop fusion | flops 1835008 | bytes 3145744 | tf_op jit(solution)/shard_map/while/body/eval_jaxpr/vmap()/reduce_sum | solution.py:82
  57.2 2.6 %copy.47 = f32[1,4,2,32,512]{4,3,2,1,0:T(8,128)S(1)} copy(f32[1,4,2,32,512]{3,2,4,1,0:T(2,128)} %bitcast.79) | data formatting | bytes 1048576 | tf_op jit(solution)/shard_map/while/body/eval_jaxpr/vmap()/stack | solution.py:84
  59.8 0.9 copy.48
  60.7 1.1 copy_dynamic-update-slice_fusion.2
  61.9 15.0 %gather_fusion = f32[16,2,32,512]{2,1,3,0:T(2,128)} fusion(f32[4,2,32,768]{2,1,0,3:T(2,128)} %bitcast.75, s32[16]{0:T(128)S(1)} %reshape.156), kind=kCustom, calls=%fused_computation.clone.1 | custom fusion | bytes 4194560 | tf_op jit(solution)/shard_map/while/body/eval_jaxpr/vmap(vmap())/gather | solution.py:43
  76.9 17.5 %select_reduce_fusion.3 = (f32[4,2,32,512]{2,1,3,0:T(2,128)S(1)}, f32[4,2,32,512]{2,1,3,0:T(2,128)}) fusion(pred[4,4]{1,0:T(4,128)(4,1)S(1)} %fusion.83, f32[16,2,32,512]{2,1,3,0:T(2,128)} %gather_fusion), kind=kLoop, calls=%fused_computation.2.clone.1 | loop fusion | flops 1835008 | bytes 3145744 | tf_op jit(solution)/shard_map/while/body/eval_jaxpr/vmap()/reduce_sum | solution.py:82
  94.4 2.6 %copy.47 = f32[1,4,2,32,512]{4,3,2,1,0:T(8,128)S(1)} copy(f32[1,4,2,32,512]{3,2,4,1,0:T(2,128)} %bitcast.79) | data formatting | bytes 1048576 | tf_op jit(solution)/shard_map/while/body/eval_jaxpr/vmap()/stack | solution.py:84
  97.0 0.9 copy.48
  97.9 1.2 copy_dynamic-update-slice_fusion.2
  99.1 72.1 %reduce-scatter.2.cloned.1.call-done = f32[1,2,2,32,512]{4,3,2,1,0:T(8,128)} async-done(((f32[8,2,2,32,512]{4,3,2,1,0:T(8,128)}), f32[1,2,2,32,512]{4,3,2,1,0:T(8,128)}) %reduce-scatter.2.cloned.1.call-update) | async-done | bytes 262160 | tf_op jit(solution)/shard_map/reduce_scatter | solution.py:87
  171.2 0.9 slice_bitcast_fusion.2
  172.2 0.7 fusion.79
  172.9 0.6 collective-permute-done.2
  173.6 0.9 fusion.56
  174.5 2.1 %collective-permute-start.3 = (f32[1,2,1,512]{3,2,1,0:T(1,128)S(1)}, f32[1,2,1,512]{3,2,1,0:T(1,128)S(1)}, u32[]{:S(2)}, u32[]{:S(2)}) collective-permute-start(f32[1,2,1,512]{3,2,1,0:T(1,128)S(1)} %get-tuple-element.156), channel_id=1, source_target_pairs={{0,1},{2,3},{4,5},{6,7},{8,9},{10,11},{12,13},{14,15},{16,17},{18,... | collective-permute-start | bytes 12296 | tf_op jit(solution)/shard_map/ppermute | solution.py:14
  176.6 1.3 collective-permute-start.4
  177.9 0.7 fusion.80
  178.5 1.1 collective-permute-done.4
  179.8 12.0 %fusion.61 = f32[1,32,512]{2,1,0:T(8,128)} fusion(f32[1,34,514]{2,1,0:T(8,128)S(1)} %get-tuple-element.155, f32[1,34,514]{2,1,0:T(8,128)S(1)} %get-tuple-element.154, f32[]{:T(128)} %bitcast.40, f32[]{:T(128)} %bitcast.39, f32[]{:T(128)} %bitcast.38, f32[]{:T(128)} %bitcast.37, f32[]{:T(128)} %bitcast.36, f32[]{:T(128)} %bitcast.35, f32[]{:T(128)} %bitcast.34, ...), kind=kLoop, calls=%fused_computation.137 | loop fusion | flops 589824 | bytes 1245256 | tf_op jit(solution)/shard_map/div | solution.py:96
  (36 shorter events, 1.6 us)
Async XLA Ops:
  6.5 5.3 %copy-start = (f32[4,5,5]{2,0,1:T(4,128)S(1)}, f32[4,5,5]{2,0,1:T(4,128)}, u32[]{:S(2)}) copy-start(f32[4,5,5]{2,0,1:T(4,128)} %param.12) | copy-start | bytes 1204
  6.5 6.9 %copy-start.2 = (s32[8,4]{0,1:T(4,128)S(1)}, s32[8,4]{0,1:T(4,128)}, u32[]{:S(2)}) copy-start(s32[8,4]{0,1:T(4,128)} %param.13) | copy-start | bytes 388
  6.5 7.0 %copy-start.3 = (s32[8,4]{0,1:T(4,128)S(1)}, s32[8,4]{0,1:T(4,128)}, u32[]{:S(2)}) copy-start(s32[8,4]{0,1:T(4,128)} %param.14) | copy-start | bytes 388
  6.5 164.7 %reduce-scatter.2.cloned.1.call-start = ((), (), s32[]{:S(2)}) async-start(), calls=%async_computation.1 | async-start | bytes 2359296 | tf_op jit(solution)/shard_map/reduce_scatter | solution.py:87
  8.2 5.4 %collective-permute-start = (f32[2,4,2,512]{3,1,2,0:T(4,128)S(1)}, f32[2,4,2,512]{3,1,2,0:T(4,128)S(1)}, u32[]{:S(2)}, u32[]{:S(2)}) collective-permute-start(f32[2,4,2,512]{3,1,2,0:T(4,128)S(1)} %get-tuple-element.150), channel_id=1, source_target_pairs={{0,1},{2,3},{4,5},{6,7},{8,9},{10,11},{12,13},{14,15},{16,17},{18,... | collective-permute-start | bytes 98312 | tf_op jit(solution)/shard_map/ppermute | solution.py:14
  10.6 3.1 %collective-permute-start.1 = (f32[2,4,2,512]{3,1,2,0:T(4,128)S(1)}, f32[2,4,2,512]{3,1,2,0:T(4,128)S(1)}, u32[]{:S(2)}, u32[]{:S(2)}) collective-permute-start(f32[2,4,2,512]{3,1,2,0:T(4,128)S(1)} %get-tuple-element.151), channel_id=1, source_target_pairs={{1,0},{3,2},{5,4},{7,6},{9,8},{11,10},{13,12},{15,14},{17,16},{19,... | collective-permute-start | bytes 98312 | tf_op jit(solution)/shard_map/ppermute | solution.py:17
  99.1 73.2 %copy-start.1 = (f32[1,3,3]{2,0,1:T(1,128)S(1)}, f32[1,3,3]{2,0,1:T(1,128)}, u32[]{:S(2)}) copy-start(f32[1,3,3]{2,0,1:T(1,128)} %param.15) | copy-start | bytes 112
  172.1 1.4 collective-permute-start.2
  174.5 4.0 %collective-permute-start.3 = (f32[1,2,1,512]{3,2,1,0:T(1,128)S(1)}, f32[1,2,1,512]{3,2,1,0:T(1,128)S(1)}, u32[]{:S(2)}, u32[]{:S(2)}) collective-permute-start(f32[1,2,1,512]{3,2,1,0:T(1,128)S(1)} %get-tuple-element.156), channel_id=1, source_target_pairs={{0,1},{2,3},{4,5},{6,7},{8,9},{10,11},{12,13},{14,15},{16,17},{18,... | collective-permute-start | bytes 12296 | tf_op jit(solution)/shard_map/ppermute | solution.py:14
  176.6 3.1 %collective-permute-start.4 = (f32[1,2,1,512]{3,2,1,0:T(1,128)S(1)}, f32[1,2,1,512]{3,2,1,0:T(1,128)S(1)}, u32[]{:S(2)}, u32[]{:S(2)}) collective-permute-start(f32[1,2,1,512]{3,2,1,0:T(1,128)S(1)} %get-tuple-element.157), channel_id=1, source_target_pairs={{1,0},{3,2},{5,4},{7,6},{9,8},{11,10},{13,12},{15,14},{17,16},{19,... | collective-permute-start | bytes 12296 | tf_op jit(solution)/shard_map/ppermute | solution.py:17
Sparse Core Ops, SparseCore 0:
  99.2 71.9 reduce-scatter.1
where the time goes:
time: 199 us
  waiting for transfers between devices  74 us (37%)
  other arithmetic  57.8 us (29%)
  local copies, waits for them, and re-layouts  46.2 us (23%)
  between operations  13.6 us (7%)
  starting transfers between devices  7.11 us (4%)
    reduce_scatter x1, waiting for transfers between devices, shards(): lax.psum_scatter(partial_value, 'expo', scatter_dimension=0, tiled=True)  72.1 us
    reduce_sum x2, other arithmetic, split_velocity(): near_sum = jnp.sum(jnp.where(select_flags, 0.0, shifted), axis=1)  35 us
    gather x4, local copies, waits for them, and re-layouts, single(): lax.dynamic_slice_in_dim(single_image, margin - pixel_shift, column_count...  30.2 us
    div x1, other arithmetic, shards(): return psi_trail / jnp.sqrt(phi_trail + 1.0)  12 us
    another operation x4, local copies, waits for them, and re-layouts, split_velocity(): return jnp.stack([near_sum, far_sum])  6.99 us
    another operation x3, other arithmetic, shards(): filtered = jnp.stack([psi_images, phi_images])  5.74 us
    ppermute x2, starting transfers between devices, padded_2(): lax.ppermute(lax.slice_in_dim(block, block.shape[dim] - width, None, axis...  4.45 us
  transfers between devices with their start and end apart: 6, of which 4 were waited for; matrix products, arithmetic and copies ran while one was open for 2% of the time, Pallas kernels for 0%

commit v1 on v0

v1 whole, which is shorter than its diff:
```python
import functools

import jax
import jax.numpy as jnp
from jax import lax
from jax.experimental import pallas as pl
from jax.experimental.pallas import tpu as pltpu
from jax.sharding import PartitionSpec as P

LANES = 128
SUB = 8
MESH = pl.DeviceIdType.MESH


def filter_rows(load, weights, taps, wide):
    sums = [None] * taps
    for a in range(taps):
        x = load(a)
        for b in range(taps):
            term = weights[a][b] * x
            sums[b] = term if sums[b] is None else sums[b] + term
    mid = taps // 2
    total = sums[mid]
    for b in range(taps):
        if b != mid:
            total = total + pltpu.roll(sums[b], (mid - b) % wide, 1)
    return total


def kernel(
    dims,
    sci, iv, msk, ps, off, shf, tk, out,
    sci_v, iv_v, msk_v, image, other, filt, part_stack,
    recv_ya, recv_yb, recv_a, recv_b, stack, trail, trail_in,
    in_sem, sky_s, sky_r, ya_s, ya_r, yb_s, yb_r, ring_s, ring_r, end_s, end_r,
):
    E, R, W, Y, Z = dims
    H = Z // 2
    taps = ps.shape[1]
    wide = W + LANES
    half_rows = R // 2
    tiles = W // LANES
    c = lax.axis_index("sky")
    me = lax.axis_index("expo")
    y = lax.rem(me, Y)
    z = me // Y
    sky = {"sky": 1 - c}
    y_peer = {"expo": z * Y + (Y - 1 - y)}
    z_peer = [
        {"expo": lax.rem(z + 1, Z) * Y + y},
        {"expo": lax.rem(z + Z - 1, Z) * Y + y},
    ]

    loads = []
    for e in range(E):
        trio = [
            pltpu.make_async_copy(src.at[e], dst.at[e], in_sem.at[n, e])
            for n, (src, dst) in enumerate(((iv, iv_v), (msk, msk_v), (sci, sci_v)))
        ]
        for copy in trio:
            copy.start()
        loads.append(trio)

    barrier = pltpu.get_barrier_semaphore()
    greeted = [sky] + ([y_peer] if Y > 1 else []) + (z_peer if Z > 1 else [])
    for peer in greeted:
        pl.semaphore_signal(barrier, inc=1, device_id=peer, device_id_type=MESH)

    top = 2 * R + SUB
    for e in range(E):
        image[e, 0:SUB, :] = jnp.zeros((SUB, wide), jnp.float32)
        image[e, top : top + SUB, :] = jnp.zeros((SUB, wide), jnp.float32)
        image[e, SUB:top, W:wide] = jnp.zeros((2 * R, LANES), jnp.float32)
        for t in range(2):
            for m in (0, tiles + 1, tiles + 2):
                filt[e, t, m] = jnp.zeros((R, LANES), jnp.float32)
    stack[0:SUB, :] = jnp.zeros((SUB, wide), jnp.float32)
    stack[top : top + SUB, :] = jnp.zeros((SUB, wide), jnp.float32)
    stack[SUB:top, W:wide] = jnp.zeros((2 * R, LANES), jnp.float32)

    own_rows = pl.ds(pl.multiple_of(SUB + R * c, SUB), R)

    def sky_copy(e):
        return pltpu.make_async_remote_copy(
            src_ref=other.at[e],
            dst_ref=image.at[e, own_rows, pl.ds(0, W)],
            send_sem=sky_s.at[e],
            recv_sem=sky_r.at[e],
            device_id=sky,
            device_id_type=MESH,
        )

    for e in range(E):
        for copy in loads[e]:
            copy.wait()
        w = iv_v[e] * msk_v[e].astype(jnp.float32)
        s = sci_v[e] * w
        image[e, own_rows, 0:W] = jnp.where(c == 0, s, w)
        other[e] = jnp.where(c == 0, w, s)
        if e == 0:
            pl.semaphore_wait(barrier, len(greeted))
        sky_copy(e).start()

    def power(value):
        return jnp.where(c == 0, value, value * value)

    def filter_one(e, carry):
        weights = [[power(ps[e, a, b]) for b in range(taps)] for a in range(taps)]
        sky_copy(e).wait_recv()
        for i in range(2 * R // SUB):
            def load(a):
                start = SUB * (i + 1) + a - taps // 2
                return image[e, start : start + SUB, :]

            total = filter_rows(load, weights, taps, wide)
            t, low = divmod(SUB * i, R)
            for k in range(tiles):
                filt[e, t, k + 1, low : low + SUB, :] = total[:, k * LANES : (k + 1) * LANES]
        return carry

    lax.fori_loop(0, E, filter_one, 0)

    lane = lax.broadcasted_iota(jnp.int32, (R, LANES), 1)

    def stack_group(zd):
        def one(j, carry):
            yy = j // 2
            t = lax.rem(j, 2)
            v = zd * Y + yy
            sums = [None] * tiles
            for e in range(E):
                o = LANES - shf[v, e]
                q = o // LANES
                r = o - q * LANES
                near = lane < LANES - r
                o_row = off[v, e]
                source = t + o_row - 2 * t * o_row
                turned = [pltpu.roll(filt[e, source, q + m], LANES - r, 1) for m in range(tiles + 1)]
                for k in range(tiles):
                    got = jnp.where(near, turned[k], turned[k + 1])
                    sums[k] = got if sums[k] is None else sums[k] + got
            for k in range(tiles):
                for p in range(2):
                    part_stack[t, zd, p, yy, :, k * LANES : (k + 1) * LANES] = sums[k][
                        half_rows * p : half_rows * (p + 1)
                    ]
            return carry

        lax.fori_loop(0, 2 * Y, one, 0)

    def ya_copy(n, zd):
        return pltpu.make_async_remote_copy(
            src_ref=part_stack.at[0, zd, :, 1 - y],
            dst_ref=recv_ya.at[n],
            send_sem=ya_s.at[n],
            recv_sem=ya_r.at[n],
            device_id=y_peer,
            device_id_type=MESH,
        )

    def yb_copy():
        return pltpu.make_async_remote_copy(
            src_ref=part_stack.at[1, z, :, 1 - y],
            dst_ref=recv_yb,
            send_sem=yb_s,
            recv_sem=yb_r,
            device_id=y_peer,
            device_id_type=MESH,
        )

    def target(way, k):
        return lax.rem(z + k, Z) if way == 0 else lax.rem(z + Z - k, Z)

    def ring_copy(half, way, k, p):
        if half == 0:
            src = part_stack.at[0, target(way, k), p, y]
            dst = recv_a.at[way, k - 1, p]
        else:
            src = part_stack.at[1, target(way, k), p]
            dst = recv_b.at[way, k - 1, p]
        return pltpu.make_async_remote_copy(
            src_ref=src,
            dst_ref=dst,
            send_sem=ring_s.at[half, way, k - 1, p],
            recv_sem=ring_r.at[half, way, k - 1, p],
            device_id=z_peer[way],
            device_id_type=MESH,
        )

    last = H if Z % 2 == 0 else (Z - 1) // 2

    def sent(way, k):
        return [way] if Z % 2 == 0 and k == last else [0, 1]

    sends = []

    def send(copy):
        copy.start()
        sends.append(copy)

    def start_fresh(half, k):
        for way in range(2):
            for p in sent(way, k):
                if k == last or (k == last - 1 and p not in sent(way, last)):
                    send(ring_copy(half, way, k, p))

    def pass_on(half):
        for k in range(last - 1, 0, -1):
            for way in range(2):
                for p in sent(way, k + 1):
                    ring_copy(half, way, k + 1, p).wait_recv()
                    if half == 0:
                        zd = target(way, k)
                        part_stack[0, zd, p, y] = part_stack[0, zd, p, y] + recv_a[way, k, p]
                    else:
                        zd = target(way, k)
                        part_stack[1, zd, p] = part_stack[1, zd, p] + recv_b[way, k, p]
                    send(ring_copy(half, way, k, p))

    groups = [(0, 0)]
    for k in range(1, last + 1):
        ways = [0] if Z % 2 == 0 and k == last else [0, 1]
        groups = [(way, k) for way in ways] + groups

    for n, (way, k) in enumerate(groups):
        zd = target(way, k)
        stack_group(zd)
        if Y > 1:
            send(ya_copy(n, zd))
        if k and (k == last or way == 1):
            start_fresh(1, k)

    pass_on(1)
    for n, (way, k) in enumerate(groups):
        zd = target(way, k)
        if Y > 1:
            ya_copy(n, zd).wait_recv()
            part_stack[0, zd, :, y] = part_stack[0, zd, :, y] + recv_ya[n]
        if k and (k == last or way == 1):
            start_fresh(0, k)
    for p in range(2):
        total = part_stack[1, z, p]
        for way in range(2):
            if last and p in sent(way, 1):
                ring_copy(1, way, 1, p).wait_recv()
                total = total + recv_b[way, 0, p]
        part_stack[1, z, p] = total
    if Y > 1:
        send(yb_copy())
    pass_on(0)
    for p in range(2):
        total = part_stack[0, z, p, y]
        for way in range(2):
            if last and p in sent(way, 1):
                ring_copy(0, way, 1, p).wait_recv()
                total = total + recv_a[way, 0, p]
        start = SUB + half_rows * p
        stack[start : start + half_rows, 0:W] = total
    if Y > 1:
        yb_copy().wait_recv()
    for p in range(2):
        start = SUB + R + half_rows * p
        total = part_stack[1, z, p, y]
        if Y > 1:
            total = total + recv_yb[p]
        stack[start : start + half_rows, 0:W] = total

    tap = tk.shape[1]
    weights = [[power(tk[0, a, b]) for b in range(tap)] for a in range(tap)]
    for i in range(2 * R // SUB):
        def load(a):
            start = SUB * (i + 1) + a - tap // 2
            return stack[start : start + SUB, :]

        trail[SUB * i : SUB * (i + 1), :] = filter_rows(load, weights, tap, wide)[:, :W]

    end = pltpu.make_async_remote_copy(
        src_ref=trail.at[pl.ds(pl.multiple_of(R * (1 - c), SUB), R)],
        dst_ref=trail_in,
        send_sem=end_s,
        recv_sem=end_r,
        device_id=sky,
        device_id_type=MESH,
    )
    send(end)
    end.wait_recv()
    mine = trail[pl.ds(pl.multiple_of(R * c, SUB), R), :]
    theirs = trail_in[...]
    psi = jnp.where(c == 0, mine, theirs)
    phi = jnp.where(c == 0, theirs, mine)
    out[0] = psi / jnp.sqrt(phi + 1.0)

    for e in range(E):
        sky_copy(e).wait_send()
    for copy in sends:
        copy.wait_send()


def shards(expo, science, inv_variance, pixel_masks, point_spread, tile_offset, column_shift, trail_kernel):
    E, R, W = science.shape
    Y = 2 if expo % 2 == 0 else 1
    Z = expo // Y
    K = max(Z // 2, 1)
    half = R // 2
    wide = W + LANES
    f32 = jnp.float32
    dma = pltpu.SemaphoreType.DMA
    hbm = pl.BlockSpec(memory_space=pl.ANY)
    smem = pl.BlockSpec(memory_space=pltpu.SMEM)
    return pl.pallas_call(
        functools.partial(kernel, (E, R, W, Y, Z)),
        out_shape=jax.ShapeDtypeStruct((1, R, W), f32),
        in_specs=[hbm] * 3 + [smem] * 4,
        out_specs=pl.BlockSpec(memory_space=pltpu.VMEM),
        scratch_shapes=[
            pltpu.VMEM((E, R, W), f32),
            pltpu.VMEM((E, R, W), f32),
            pltpu.VMEM((E, R, W), jnp.int32),
            pltpu.VMEM((E, 2 * R + 2 * SUB, wide), f32),
            pltpu.VMEM((E, R, W), f32),
            pltpu.VMEM((E, 2, W // LANES + 3, R, LANES), f32),
            pltpu.VMEM((2, Z, 2, Y, half, W), f32),
            pltpu.VMEM((Z, 2, half, W), f32),
            pltpu.VMEM((2, half, W), f32),
            pltpu.VMEM((2, K, 2, half, W), f32),
            pltpu.VMEM((2, K, 2, Y, half, W), f32),
            pltpu.VMEM((2 * R + 2 * SUB, wide), f32),
            pltpu.VMEM((2 * R, W), f32),
            pltpu.VMEM((R, W), f32),
            dma((3, E)),
            dma((E,)),
            dma((E,)),
            dma((Z,)),
            dma((Z,)),
            dma,
            dma,
            dma((2, 2, K, 2)),
            dma((2, 2, K, 2)),
            dma,
            dma,
        ],
        compiler_params=pltpu.CompilerParams(collective_id=0, has_side_effects=True),
    )(science, inv_variance, pixel_masks, point_spread, tile_offset, column_shift, trail_kernel)


def solution(mesh):
    return jax.shard_map(
        functools.partial(shards, mesh.shape["expo"]),
        mesh=mesh,
        in_specs=(
            P(("field", "expo"), "sky", None),
            P(("field", "expo"), "sky", None),
            P(("field", "expo"), "sky", None),
            P(("field", "expo"), None, None),
            P(None, "expo"),
            P(None, "expo"),
            P("expo", None, None),
        ),
        out_specs=P(("field", "expo"), "sky", None),
        check_vma=False,
    )
```

time: 199 us -> 34.3 us (0.17)
  waiting for transfers between devices: 74 us -> 0 us
  other arithmetic: 57.8 us -> 0 us
  local copies, waits for them, and re-layouts: 46.2 us -> 5.4 us
  Pallas kernels: 0 us -> 28.5 us
  between operations: 13.6 us -> 0.01 us
  starting transfers between devices: 7.11 us -> 0 us
    reduce_scatter x1 -> x0, waiting for transfers between devices: 72.1 us -> none  [shards(): lax.psum_scatter(partial_value, 'expo', scatter_dimension=0, tiled=True)]
    reduce_sum x2 -> x0, other arithmetic: 35 us -> none  [split_velocity(): near_sum = jnp.sum(jnp.where(select_flags, 0.0, shifted), axis=1)]
    gather x4 -> x0, local copies, waits for them, and re-layouts: 30.2 us -> none  [single(): lax.dynamic_slice_in_dim(single_image, margin - pixel_shift, column_count...]
    pallas_call x0 -> x1, Pallas kernels: none -> 28.5 us  [shards(): pl.pallas_call(functools.partial(kernel, (E, R, W, Y, Z)), out_shape=jax....]
    div x1 -> x0, other arithmetic: 12 us -> none  [shards(): return psi_trail / jnp.sqrt(phi_trail + 1.0)]
    another operation x7 -> x0, local copies, waits for them, and re-layouts: 7.51 us -> none  [the longest x4 6.99 us: split_velocity(): return jnp.stack([near_sum, far_sum])]
    ppermute x5 -> x0, starting transfers between devices: 7.11 us -> none  [the longest x2 4.45 us: padded_2(): lax.ppermute(lax.slice_in_dim(block, block.shape[dim] - width, None, axis...]
    another operation x5 -> x0, other arithmetic: 6.99 us -> none  [the longest x3 5.74 us: shards(): filtered = jnp.stack([psi_images, phi_images])]
  transfers between devices with their start and end apart: 6 -> 0, of which waited for: 4 -> 0; matrix products, arithmetic and copies ran while one was open for 2% -> 0% of each run, Pallas kernels for 0% -> 0%
where the time goes in v1:
time: 34.3 us; the launch traced here: 33.9 us
  Pallas kernels  28.5 us (83%)
  local copies, waits for them, and re-layouts  5.4 us (16%)
    pallas_call x1, Pallas kernels, shards(): pl.pallas_call(functools.partial(kernel, (E, R, W, Y, Z)), out_shape=jax....  28.5 us
    unnamed x9, local copies, waits for them, and re-layouts  5.4 us

profile of v1, /device:TPU:0, one launch (start us, length us, event | category | flops | bytes accessed | tf_op | source)
XLA Modules:
  0.0 33.9 jit_solution(15503525384851838579)
XLA Ops:
  0.0 0.0 copy-start.1
  0.0 0.0 copy-start
  0.0 1.3 %copy.11.tk = f32[1,3,3]{2,1,0:T(4,128)} copy(f32[1,3,3]{2,0,1:T(1,128)} %param.13) | data formatting | bytes 72 | tf_op args[6]
  1.3 0.0 copy-done.1
  1.3 0.7 %copy.9.off = s32[8,4]{1,0:T(8,128)} copy(s32[8,4]{0,1:T(4,128)S(1)} %copy-done.1) | data formatting | bytes 256 | tf_op args[4]
  2.0 1.3 %copy.10.shf = s32[8,4]{1,0:T(8,128)} copy(s32[8,4]{0,1:T(4,128)} %param.12) | data formatting | bytes 256 | tf_op args[5]
  3.3 0.0 copy-done
  3.3 0.6 %copy.8.ps = f32[4,5,5]{2,1,0:T(8,128)} copy(f32[4,5,5]{2,0,1:T(4,128)S(1)} %copy-done) | data formatting | bytes 800 | tf_op args[3]
  3.9 28.5 %shard_map.73 = f32[1,32,512]{2,1,0:T(8,128)} custom-call(f32[4,32,512]{2,1,0:T(8,128)} %sci.1, f32[4,32,512]{2,1,0:T(8,128)} %iv.1, s32[4,32,512]{2,1,0:T(8,128)} %msk.1, f32[4,5,5]{2,1,0:T(8,128)} %copy.8.ps, s32[8,4]{1,0:T(8,128)} %copy.9.off, s32[8,4]{1,0:T(8,128)} %copy.10.shf, f32[1,3,3]{2,1,0:T(4,128)} %copy.11.tk), custom_call_target="tpu_custom_call" | custom-call | tf_op jit(solution)/shard_map/pallas_call | solution.py:310
  32.5 1.5 %copy.13 = f32[1,32,512]{2,1,0:T(8,128)} copy(f32[1,32,512]{2,1,0:T(8,128)} %shard_map.73) | data formatting | bytes 131072
Async XLA Ops:
  0.0 1.3 %copy-start.1 = (s32[8,4]{0,1:T(4,128)S(1)}, s32[8,4]{0,1:T(4,128)}, u32[]{:S(2)}) copy-start(s32[8,4]{0,1:T(4,128)} %param.11) | copy-start | bytes 388
  0.0 3.3 %copy-start = (f32[4,5,5]{2,0,1:T(4,128)S(1)}, f32[4,5,5]{2,0,1:T(4,128)}, u32[]{:S(2)}) copy-start(f32[4,5,5]{2,0,1:T(4,128)} %param.10) | copy-start | bytes 1204

commit v2 on v1

v2 whole, which is shorter than its diff:
```python
import functools

import jax
import jax.numpy as jnp
from jax import lax
from jax.experimental import pallas as pl
from jax.experimental.pallas import tpu as pltpu
from jax.sharding import PartitionSpec as P

LANES = 128
SUB = 8
FIRST = 3
MESH = pl.DeviceIdType.MESH


def filter_rows(load, weights, taps, wide):
    sums = [None] * taps
    for a in range(taps):
        x = load(a)
        for b in range(taps):
            term = weights[a][b] * x
            sums[b] = term if sums[b] is None else sums[b] + term
    mid = taps // 2
    total = sums[mid]
    for b in range(taps):
        if b != mid:
            total = total + pltpu.roll(sums[b], (mid - b) % wide, 1)
    return total


def kernel(
    dims,
    sci, iv, msk, ps, off, shf, tk, out,
    sci_v, iv_v, msk_v, image, other, filt, part_stack,
    recv_ya, recv_yb, recv_a, recv_b, stack, trail, trail_in,
    in_sem, sky_s, sky_r, ya_s, ya_r, yb_s, yb_r, line_s, line_r, end_s, end_r,
):
    E, R, W, Y, Z = dims
    taps = ps.shape[0]
    wide = W + LANES
    band = R // 2
    tiles = W // LANES
    c = lax.axis_index("sky")
    me = lax.axis_index("expo")
    y = lax.rem(me, Y)
    z = me // Y
    sky = {"sky": 1 - c}
    y_peer = {"expo": z * Y + (Y - 1 - y)}
    loads = []
    for e in range(E):
        trio = [
            pltpu.make_async_copy(src.at[e], dst.at[e], in_sem.at[n, e])
            for n, (src, dst) in enumerate(((iv, iv_v), (msk, msk_v), (sci, sci_v)))
        ]
        for copy in trio:
            copy.start()
        loads.append(trio)

    barrier = pltpu.get_barrier_semaphore()
    for peer in [sky] + ([y_peer] if Y > 1 else []):
        pl.semaphore_signal(barrier, inc=1, device_id=peer, device_id_type=MESH)

    @pl.when(z > 0)
    def _():
        pl.semaphore_signal(barrier, inc=1, device_id={"expo": me - Y}, device_id_type=MESH)

    @pl.when(z < Z - 1)
    def _():
        pl.semaphore_signal(barrier, inc=1, device_id={"expo": me + Y}, device_id_type=MESH)

    greeted = (2 if Y > 1 else 1) + jnp.where(z > 0, 1, 0) + jnp.where(z < Z - 1, 1, 0)

    top = 2 * R + SUB
    for e in range(E):
        image[e, 0:SUB, :] = jnp.zeros((SUB, wide), jnp.float32)
        image[e, top : top + SUB, :] = jnp.zeros((SUB, wide), jnp.float32)
        image[e, SUB:top, W:wide] = jnp.zeros((2 * R, LANES), jnp.float32)
        for t in range(2):
            for m in (0, tiles + 1, tiles + 2):
                filt[e, t, m] = jnp.zeros((R, LANES), jnp.float32)
    stack[0:SUB, :] = jnp.zeros((SUB, wide), jnp.float32)
    stack[top : top + SUB, :] = jnp.zeros((SUB, wide), jnp.float32)
    stack[SUB:top, W:wide] = jnp.zeros((2 * R, LANES), jnp.float32)

    own_rows = pl.ds(pl.multiple_of(SUB + R * c, SUB), R)

    def sky_copy(e):
        return pltpu.make_async_remote_copy(
            src_ref=other.at[e],
            dst_ref=image.at[e, own_rows, pl.ds(0, W)],
            send_sem=sky_s.at[e],
            recv_sem=sky_r.at[e],
            device_id=sky,
            device_id_type=MESH,
        )

    for e in range(E):
        for copy in loads[e]:
            copy.wait()
        w = iv_v[e] * msk_v[e].astype(jnp.float32)
        s = sci_v[e] * w
        image[e, own_rows, 0:W] = jnp.where(c == 0, s, w)
        other[e] = jnp.where(c == 0, w, s)
        if e == 0:
            pl.semaphore_wait(barrier, greeted)
        sky_copy(e).start()

    def power(value):
        return jnp.where(c == 0, value, value * value)

    def filter_one(e, carry):
        weights = [[power(ps[a, e, b]) for b in range(taps)] for a in range(taps)]
        sky_copy(e).wait_recv()
        for i in range(2 * R // SUB):
            def load(a):
                start = SUB * (i + 1) + a - taps // 2
                return image[e, start : start + SUB, :]

            total = filter_rows(load, weights, taps, wide)
            t, low = divmod(SUB * i, R)
            for k in range(tiles):
                filt[e, t, k + 1, low : low + SUB, :] = total[:, k * LANES : (k + 1) * LANES]
        return carry

    lax.fori_loop(0, E, filter_one, 0)

    lane = lax.broadcasted_iota(jnp.int32, (R, LANES), 1)

    def stack_group(zd):
        def one(yy, carry):
            v = zd * Y + yy
            sums = [[None] * tiles for _ in range(2)]
            for e in range(E):
                o = LANES - shf[e, v]
                q = o // LANES
                r = o - q * LANES
                near = lane < LANES - r
                o_row = off[e, v]
                for t in range(2):
                    source = t + o_row - 2 * t * o_row
                    turned = [pltpu.roll(filt[e, source, q + m], LANES - r, 1) for m in range(tiles + 1)]
                    for k in range(tiles):
                        got = jnp.where(near, turned[k], turned[k + 1])
                        sums[t][k] = got if sums[t][k] is None else sums[t][k] + got
            for t in range(2):
                for k in range(tiles):
                    for p in range(2):
                        rows = sums[t][k][band * p : band * (p + 1)]
                        part_stack[zd, 2 * t + p, yy, :, k * LANES : (k + 1) * LANES] = rows
            return carry

        lax.fori_loop(0, Y, one, 0)

    def ya_copy(n):
        return pltpu.make_async_remote_copy(
            src_ref=part_stack.at[order(n), pl.ds(0, FIRST), 1 - y],
            dst_ref=recv_ya.at[n],
            send_sem=ya_s.at[n],
            recv_sem=ya_r.at[n],
            device_id=y_peer,
            device_id_type=MESH,
        )

    def yb_copy():
        return pltpu.make_async_remote_copy(
            src_ref=part_stack.at[z, FIRST, 1 - y],
            dst_ref=recv_yb,
            send_sem=yb_s,
            recv_sem=yb_r,
            device_id=y_peer,
            device_id_type=MESH,
        )

    def order(n):
        return jnp.where(2 * z < Z, Z - 1 - n, n)

    def line_copy(way, d, g):
        if g < FIRST:
            src = part_stack.at[d, g, y]
            dst = recv_a.at[way, d, g]
        else:
            src = part_stack.at[d, g]
            dst = recv_b.at[way, d]
        return pltpu.make_async_remote_copy(
            src_ref=src,
            dst_ref=dst,
            send_sem=line_s.at[way, d, g],
            recv_sem=line_r.at[way, d, g],
            device_id={"expo": me + Y * (1 - 2 * way)},
            device_id_type=MESH,
        )

    def take(way, d, g):
        line_copy(way, d, g).wait_recv()
        if g < FIRST:
            part_stack[d, g, y] = part_stack[d, g, y] + recv_a[way, d, g]
        else:
            part_stack[d, g] = part_stack[d, g] + recv_b[way, d]

    def pass_on(n, g):
        d = order(n)
        way = jnp.where(d > z, 0, 1)

        @pl.when(d != z)
        def _():
            @pl.when((1 - way) * z + way * (Z - 1 - z) > 0)
            def _():
                take(way, d, g)

            line_copy(way, d, g).start()

    def finish(g):
        @pl.when(z > 0)
        def _():
            take(0, z, g)

        @pl.when(z < Z - 1)
        def _():
            take(1, z, g)

    for n in range(Z):
        stack_group(order(n))
        if Y > 1:
            ya_copy(n).start()

        @pl.when((z == 0) | (z == Z - 1))
        def _():
            pass_on(n, FIRST)

    @pl.when((z > 0) & (z < Z - 1))
    def _():
        for n in range(Z):
            pass_on(n, FIRST)

    for n in range(Z):
        if Y > 1:
            d = order(n)
            ya_copy(n).wait_recv()
            part_stack[d, 0:FIRST, y] = part_stack[d, 0:FIRST, y] + recv_ya[n]
        for g in range(FIRST):
            pass_on(n, g)
    finish(FIRST)
    if Y > 1:
        yb_copy().start()
    for g in range(FIRST):
        finish(g)
        start = SUB + band * g
        stack[start : start + band, 0:W] = part_stack[z, g, y]
    start = SUB + band * FIRST
    if Y > 1:
        yb_copy().wait_recv()
        stack[start : start + band, 0:W] = part_stack[z, FIRST, y] + recv_yb[...]
    else:
        stack[start : start + band, 0:W] = part_stack[z, FIRST, y]

    tap = tk.shape[0]
    weights = [[power(tk[a, 0, b]) for b in range(tap)] for a in range(tap)]
    for i in range(2 * R // SUB):
        def load(a):
            start = SUB * (i + 1) + a - tap // 2
            return stack[start : start + SUB, :]

        trail[SUB * i : SUB * (i + 1), :] = filter_rows(load, weights, tap, wide)[:, :W]

    end = pltpu.make_async_remote_copy(
        src_ref=trail.at[pl.ds(pl.multiple_of(R * (1 - c), SUB), R)],
        dst_ref=trail_in,
        send_sem=end_s,
        recv_sem=end_r,
        device_id=sky,
        device_id_type=MESH,
    )
    end.start()
    end.wait_recv()
    mine = trail[pl.ds(pl.multiple_of(R * c, SUB), R), :]
    theirs = trail_in[...]
    psi = jnp.where(c == 0, mine, theirs)
    phi = jnp.where(c == 0, theirs, mine)
    out[0] = psi / jnp.sqrt(phi + 1.0)

    for e in range(E):
        sky_copy(e).wait_send()
    end.wait_send()
    if Y > 1:
        yb_copy().wait_send()
        for n in range(Z):
            ya_copy(n).wait_send()
    for n in range(Z):
        d = order(n)

        @pl.when(d != z)
        def _():
            for g in range(FIRST + 1):
                line_copy(jnp.where(d > z, 0, 1), d, g).wait_send()


def shards(expo, science, inv_variance, pixel_masks, point_spread, tile_offset, column_shift, trail_kernel):
    E, R, W = science.shape
    Y = 2 if expo % 2 == 0 else 1
    Z = expo // Y
    band = R // 2
    wide = W + LANES
    f32 = jnp.float32
    dma = pltpu.SemaphoreType.DMA
    hbm = pl.BlockSpec(memory_space=pl.ANY)
    smem = pl.BlockSpec(memory_space=pltpu.SMEM)
    return pl.pallas_call(
        functools.partial(kernel, (E, R, W, Y, Z)),
        out_shape=jax.ShapeDtypeStruct((1, R, W), f32),
        in_specs=[hbm] * 3 + [smem] * 4,
        out_specs=pl.BlockSpec(memory_space=pltpu.VMEM),
        scratch_shapes=[
            pltpu.VMEM((E, R, W), f32),
            pltpu.VMEM((E, R, W), f32),
            pltpu.VMEM((E, R, W), jnp.int32),
            pltpu.VMEM((E, 2 * R + 2 * SUB, wide), f32),
            pltpu.VMEM((E, R, W), f32),
            pltpu.VMEM((E, 2, W // LANES + 3, R, LANES), f32),
            pltpu.VMEM((Z, FIRST + 1, Y, band, W), f32),
            pltpu.VMEM((Z, FIRST, band, W), f32),
            pltpu.VMEM((band, W), f32),
            pltpu.VMEM((2, Z, FIRST, band, W), f32),
            pltpu.VMEM((2, Z, Y, band, W), f32),
            pltpu.VMEM((2 * R + 2 * SUB, wide), f32),
            pltpu.VMEM((2 * R, W), f32),
            pltpu.VMEM((R, W), f32),
            dma((3, E)),
            dma((E,)),
            dma((E,)),
            dma((Z,)),
            dma((Z,)),
            dma,
            dma,
            dma((2, Z, FIRST + 1)),
            dma((2, Z, FIRST + 1)),
            dma,
            dma,
        ],
        compiler_params=pltpu.CompilerParams(collective_id=0, has_side_effects=True),
    )(
        science,
        inv_variance,
        pixel_masks,
        jnp.transpose(point_spread, (1, 0, 2)),
        tile_offset.T,
        column_shift.T,
        jnp.transpose(trail_kernel, (1, 0, 2)),
    )


def solution(mesh):
    return jax.shard_map(
        functools.partial(shards, mesh.shape["expo"]),
        mesh=mesh,
        in_specs=(
            P(("field", "expo"), "sky", None),
            P(("field", "expo"), "sky", None),
            P(("field", "expo"), "sky", None),
            P(("field", "expo"), None, None),
            P(None, "expo"),
            P(None, "expo"),
            P("expo", None, None),
        ),
        out_specs=P(("field", "expo"), "sky", None),
        check_vma=False,
    )
```

time: 34.3 us -> 29.6 us (0.86)
  local copies, waits for them, and re-layouts: 5.4 us -> 1.47 us
  Pallas kernels: 28.5 us -> 27.8 us
    unnamed x9 -> x1, local copies, waits for them, and re-layouts: 5.4 us -> 1.47 us
    pallas_call x1, Pallas kernels: 28.5 us -> 27.8 us  [shards(): pl.pallas_call(functools.partial(kernel, (E, R, W, Y, Z)), out_shape=jax....]
where the time goes in v2:
time: 29.6 us; the launch traced here: 29.3 us
  Pallas kernels  27.8 us (94%)
  local copies, waits for them, and re-layouts  1.47 us (5%)
    pallas_call x1, Pallas kernels, shards(): pl.pallas_call(functools.partial(kernel, (E, R, W, Y, Z)), out_shape=jax....  27.8 us
    unnamed x1, local copies, waits for them, and re-layouts  1.47 us

profile of v2, /device:TPU:0, one launch (start us, length us, event | category | flops | bytes accessed | tf_op | source)
XLA Modules:
  0.0 29.3 jit_solution(12051366731362446203)
XLA Ops:
  0.0 27.8 %shard_map.73 = f32[1,32,512]{2,1,0:T(8,128)} custom-call(f32[4,32,512]{2,1,0:T(8,128)} %sci.1, f32[4,32,512]{2,1,0:T(8,128)} %iv.1, s32[4,32,512]{2,1,0:T(8,128)} %msk.1, f32[5,4,5]{2,1,0:T(4,128)} %bitcast.4, s32[4,8]{1,0:T(4,128)} %bitcast.5, s32[4,8]{1,0:T(4,128)} %bitcast.6, f32[3,1,3]{2,1,0:T(1,128)} %bitcast.7), custom_call_target="tpu_custom_call" | custom-call | tf_op jit(solution)/shard_map/pallas_call | solution.py:307
  27.8 1.5 %copy.9 = f32[1,32,512]{2,1,0:T(8,128)} copy(f32[1,32,512]{2,1,0:T(8,128)} %shard_map.73) | data formatting | bytes 131072

commit v3 on v2

--- a/solution.py
+++ b/solution.py
@@ -13,7 +13,7 @@
 MESH = pl.DeviceIdType.MESH
 
 
-def filter_rows(load, weights, taps, wide):
+def filter_rows(load, weights, taps):
     sums = [None] * taps
     for a in range(taps):
         x = load(a)
@@ -21,23 +21,34 @@
             term = weights[a][b] * x
             sums[b] = term if sums[b] is None else sums[b] + term
     mid = taps // 2
-    total = sums[mid]
+    width = sums[0].shape[1]
+    tiles = width // LANES
+    lane = lax.broadcasted_iota(jnp.int32, (sums[0].shape[0], LANES), 1)
+    total = [sums[mid][:, LANES * k : LANES * (k + 1)] for k in range(tiles)]
     for b in range(taps):
-        if b != mid:
-            total = total + pltpu.roll(sums[b], (mid - b) % wide, 1)
+        if b == mid:
+            continue
+        turned = pltpu.roll(sums[b], (mid - b) % width, 1)
+        for k in range(tiles):
+            piece = turned[:, LANES * k : LANES * (k + 1)]
+            if b < mid and k == 0:
+                piece = jnp.where(lane >= mid - b, piece, 0.0)
+            if b > mid and k == tiles - 1:
+                piece = jnp.where(lane < LANES - (b - mid), piece, 0.0)
+            total[k] = total[k] + piece
     return total
 
 
 def kernel(
     dims,
-    sci, iv, msk, ps, off, shf, tk, out,
+    sci, iv, msk, ps_in, off_in, shf_in, tk_in, out,
+    ps, off, shf, tk,
     sci_v, iv_v, msk_v, image, other, filt, part_stack,
     recv_ya, recv_yb, recv_a, recv_b, stack, trail, trail_in,
-    in_sem, sky_s, sky_r, ya_s, ya_r, yb_s, yb_r, line_s, line_r, end_s, end_r,
+    in_sem, small_sem, sky_s, sky_r, ya_s, ya_r, yb_s, yb_r, line_s, line_r, end_s, end_r,
 ):
     E, R, W, Y, Z = dims
     taps = ps.shape[0]
-    wide = W + LANES
     band = R // 2
     tiles = W // LANES
     c = lax.axis_index("sky")
@@ -46,6 +57,20 @@
     z = me // Y
     sky = {"sky": 1 - c}
     y_peer = {"expo": z * Y + (Y - 1 - y)}
+    barrier = pltpu.get_barrier_semaphore()
+    for peer in [sky] + ([y_peer] if Y > 1 else []):
+        pl.semaphore_signal(barrier, inc=1, device_id=peer, device_id_type=MESH)
+
+    @pl.when(z > 0)
+    def _():
+        pl.semaphore_signal(barrier, inc=1, device_id={"expo": me - Y}, device_id_type=MESH)
+
+    @pl.when(z < Z - 1)
+    def _():
+        pl.semaphore_signal(barrier, inc=1, device_id={"expo": me + Y}, device_id_type=MESH)
+
+    greeted = (2 if Y > 1 else 1) + jnp.where(z > 0, 1, 0) + jnp.where(z < Z - 1, 1, 0)
+
     loads = []
     for e in range(E):
         trio = [
@@ -56,31 +81,22 @@
             copy.start()
         loads.append(trio)
 
-    barrier = pltpu.get_barrier_semaphore()
-    for peer in [sky] + ([y_peer] if Y > 1 else []):
-        pl.semaphore_signal(barrier, inc=1, device_id=peer, device_id_type=MESH)
-
-    @pl.when(z > 0)
-    def _():
-        pl.semaphore_signal(barrier, inc=1, device_id={"expo": me - Y}, device_id_type=MESH)
-
-    @pl.when(z < Z - 1)
-    def _():
-        pl.semaphore_signal(barrier, inc=1, device_id={"expo": me + Y}, device_id_type=MESH)
-
-    greeted = (2 if Y > 1 else 1) + jnp.where(z > 0, 1, 0) + jnp.where(z < Z - 1, 1, 0)
+    small = [
+        pltpu.make_async_copy(src, dst, small_sem.at[n])
+        for n, (src, dst) in enumerate(((ps_in, ps), (off_in, off), (shf_in, shf), (tk_in, tk)))
+    ]
+    for copy in small:
+        copy.start()
 
     top = 2 * R + SUB
     for e in range(E):
-        image[e, 0:SUB, :] = jnp.zeros((SUB, wide), jnp.float32)
-        image[e, top : top + SUB, :] = jnp.zeros((SUB, wide), jnp.float32)
-        image[e, SUB:top, W:wide] = jnp.zeros((2 * R, LANES), jnp.float32)
+        image[e, 0:SUB, :] = jnp.zeros((SUB, W), jnp.float32)
+        image[e, top : top + SUB, :] = jnp.zeros((SUB, W), jnp.float32)
         for t in range(2):
             for m in (0, tiles + 1, tiles + 2):
                 filt[e, t, m] = jnp.zeros((R, LANES), jnp.float32)
-    stack[0:SUB, :] = jnp.zeros((SUB, wide), jnp.float32)
-    stack[top : top + SUB, :] = jnp.zeros((SUB, wide), jnp.float32)
-    stack[SUB:top, W:wide] = jnp.zeros((2 * R, LANES), jnp.float32)
+    stack[0:SUB, :] = jnp.zeros((SUB, W), jnp.float32)
+    stack[top : top + SUB, :] = jnp.zeros((SUB, W), jnp.float32)
 
     own_rows = pl.ds(pl.multiple_of(SUB + R * c, SUB), R)
 
@@ -101,28 +117,47 @@
         s = sci_v[e] * w
         image[e, own_rows, 0:W] = jnp.where(c == 0, s, w)
         other[e] = jnp.where(c == 0, w, s)
-        if e == 0:
-            pl.semaphore_wait(barrier, greeted)
-        sky_copy(e).start()
 
     def power(value):
         return jnp.where(c == 0, value, value * value)
 
-    def filter_one(e, carry):
+    def filter_chunks(e, chunks):
         weights = [[power(ps[a, e, b]) for b in range(taps)] for a in range(taps)]
-        sky_copy(e).wait_recv()
-        for i in range(2 * R // SUB):
+        for i in chunks:
             def load(a):
                 start = SUB * (i + 1) + a - taps // 2
                 return image[e, start : start + SUB, :]
 
-            total = filter_rows(load, weights, taps, wide)
             t, low = divmod(SUB * i, R)
-            for k in range(tiles):
-                filt[e, t, k + 1, low : low + SUB, :] = total[:, k * LANES : (k + 1) * LANES]
+            for k, piece in enumerate(filter_rows(load, weights, taps)):
+                filt[e, t, k + 1, low : low + SUB, :] = piece
+
+    for copy in small:
+        copy.wait()
+    chunks = R // SUB
+    own_chunks = (range(0, chunks - 1), range(chunks + 1, 2 * chunks))
+    late_chunks = (range(chunks - 1, 2 * chunks), range(0, chunks + 1))
+
+    def own_filter(e, carry):
+        for side in range(2):
+            @pl.when(c == side)
+            def _():
+                filter_chunks(e, own_chunks[side])
         return carry
 
-    lax.fori_loop(0, E, filter_one, 0)
+    def late_filter(e, carry):
+        sky_copy(e).wait_recv()
+        for side in range(2):
+            @pl.when(c == side)
+            def _():
+                filter_chunks(e, late_chunks[side])
+        return carry
+
+    lax.fori_loop(0, E, own_filter, 0)
+    pl.semaphore_wait(barrier, greeted)
+    for e in range(E):
+        sky_copy(e).start()
+    lax.fori_loop(0, E, late_filter, 0)
 
     lane = lax.broadcasted_iota(jnp.int32, (R, LANES), 1)
 
@@ -260,7 +295,8 @@
             start = SUB * (i + 1) + a - tap // 2
             return stack[start : start + SUB, :]
 
-        trail[SUB * i : SUB * (i + 1), :] = filter_rows(load, weights, tap, wide)[:, :W]
+        for k, piece in enumerate(filter_rows(load, weights, tap)):
+            trail[SUB * i : SUB * (i + 1), LANES * k : LANES * (k + 1)] = piece
 
     end = pltpu.make_async_remote_copy(
         src_ref=trail.at[pl.ds(pl.multiple_of(R * (1 - c), SUB), R)],
@@ -299,21 +335,24 @@
     Y = 2 if expo % 2 == 0 else 1
     Z = expo // Y
     band = R // 2
-    wide = W + LANES
+    taps = point_spread.shape[1]
     f32 = jnp.float32
     dma = pltpu.SemaphoreType.DMA
     hbm = pl.BlockSpec(memory_space=pl.ANY)
-    smem = pl.BlockSpec(memory_space=pltpu.SMEM)
     return pl.pallas_call(
         functools.partial(kernel, (E, R, W, Y, Z)),
         out_shape=jax.ShapeDtypeStruct((1, R, W), f32),
-        in_specs=[hbm] * 3 + [smem] * 4,
+        in_specs=[hbm] * 7,
         out_specs=pl.BlockSpec(memory_space=pltpu.VMEM),
         scratch_shapes=[
+            pltpu.SMEM((taps, E, taps), f32),
+            pltpu.SMEM(tile_offset.shape[::-1], jnp.int32),
+            pltpu.SMEM(column_shift.shape[::-1], jnp.int32),
+            pltpu.SMEM((trail_kernel.shape[1], 1, trail_kernel.shape[2]), f32),
             pltpu.VMEM((E, R, W), f32),
             pltpu.VMEM((E, R, W), f32),
             pltpu.VMEM((E, R, W), jnp.int32),
-            pltpu.VMEM((E, 2 * R + 2 * SUB, wide), f32),
+            pltpu.VMEM((E, 2 * R + 2 * SUB, W), f32),
             pltpu.VMEM((E, R, W), f32),
             pltpu.VMEM((E, 2, W // LANES + 3, R, LANES), f32),
             pltpu.VMEM((Z, FIRST + 1, Y, band, W), f32),
@@ -321,10 +360,11 @@
             pltpu.VMEM((band, W), f32),
             pltpu.VMEM((2, Z, FIRST, band, W), f32),
             pltpu.VMEM((2, Z, Y, band, W), f32),
-            pltpu.VMEM((2 * R + 2 * SUB, wide), f32),
+            pltpu.VMEM((2 * R + 2 * SUB, W), f32),
             pltpu.VMEM((2 * R, W), f32),
             pltpu.VMEM((R, W), f32),
             dma((3, E)),
+            dma((4,)),
             dma((E,)),
             dma((E,)),
             dma((Z,)),

time: 29.6 us -> 28.5 us (0.963)
  Pallas kernels: 27.8 us -> 26.8 us
    pallas_call x1, Pallas kernels: 27.8 us -> 26.8 us  [shards(): pl.pallas_call(functools.partial(kernel, (E, R, W, Y, Z)), out_shape=jax....]
where the time goes in v3:
time: 28.5 us; the launch traced here: 28.3 us
  Pallas kernels  26.8 us (94%)
  local copies, waits for them, and re-layouts  1.47 us (5%)
    pallas_call x1, Pallas kernels, shards(): pl.pallas_call(functools.partial(kernel, (E, R, W, Y, Z)), out_shape=jax....  26.8 us
    unnamed x1, local copies, waits for them, and re-layouts  1.47 us

profile of v3, /device:TPU:0, one launch (start us, length us, event | category | flops | bytes accessed | tf_op | source)
XLA Modules:
  0.0 28.3 jit_solution(13945572271763286444)
XLA Ops:
  0.0 26.8 %shard_map.73 = f32[1,32,512]{2,1,0:T(8,128)} custom-call(f32[4,32,512]{2,1,0:T(8,128)} %sci.1, f32[4,32,512]{2,1,0:T(8,128)} %iv.1, s32[4,32,512]{2,1,0:T(8,128)} %msk.1, f32[5,4,5]{2,1,0:T(4,128)} %bitcast.4, s32[4,8]{1,0:T(4,128)} %bitcast.5, s32[4,8]{1,0:T(4,128)} %bitcast.6, f32[3,1,3]{2,1,0:T(1,128)} %bitcast.7), custom_call_target="tpu_custom_call" | custom-call | tf_op jit(solution)/shard_map/pallas_call | solution.py:342
  26.8 1.5 %copy.9 = f32[1,32,512]{2,1,0:T(8,128)} copy(f32[1,32,512]{2,1,0:T(8,128)} %shard_map.73) | data formatting | bytes 131072

commit v4 on v3

--- a/solution.py
+++ b/solution.py
@@ -341,7 +341,7 @@
     hbm = pl.BlockSpec(memory_space=pl.ANY)
     return pl.pallas_call(
         functools.partial(kernel, (E, R, W, Y, Z)),
-        out_shape=jax.ShapeDtypeStruct((1, R, W), f32),
+        out_shape=pltpu.VMEM((1, R, W), f32),
         in_specs=[hbm] * 7,
         out_specs=pl.BlockSpec(memory_space=pltpu.VMEM),
         scratch_shapes=[

time: 28.5 us -> 27 us (0.947)
  local copies, waits for them, and re-layouts: 1.47 us -> 0.63 us
  Pallas kernels: 26.8 us -> 26.2 us
    unnamed x1, local copies, waits for them, and re-layouts: 1.47 us -> 0.63 us
    pallas_call x1, Pallas kernels: 26.8 us -> 26.2 us  [shards(): pl.pallas_call(functools.partial(kernel, (E, R, W, Y, Z)), out_shape=pltp...]
where the time goes in v4:
time: 27 us; the launch traced here: 26.8 us
  Pallas kernels  26.2 us (97%)
  local copies, waits for them, and re-layouts  0.63 us (2%)
    pallas_call x1, Pallas kernels, shards(): pl.pallas_call(functools.partial(kernel, (E, R, W, Y, Z)), out_shape=pltp...  26.2 us
    unnamed x1, local copies, waits for them, and re-layouts  0.63 us

profile of v4, /device:TPU:0, one launch (start us, length us, event | category | flops | bytes accessed | tf_op | source)
XLA Modules:
  0.0 26.8 jit_solution(15123351626469835043)
XLA Ops:
  0.0 26.2 %shard_map.73 = f32[1,32,512]{2,1,0:T(8,128)S(1)} custom-call(f32[4,32,512]{2,1,0:T(8,128)} %sci.1, f32[4,32,512]{2,1,0:T(8,128)} %iv.1, s32[4,32,512]{2,1,0:T(8,128)} %msk.1, f32[5,4,5]{2,1,0:T(4,128)} %bitcast.4, s32[4,8]{1,0:T(4,128)} %bitcast.5, s32[4,8]{1,0:T(4,128)} %bitcast.6, f32[3,1,3]{2,1,0:T(1,128)} %bitcast.7), custom_call_target="tpu_custom_call" | custom-call | tf_op jit(solution)/shard_map/pallas_call | solution.py:342
  26.2 0.6 %copy.9 = f32[1,32,512]{2,1,0:T(8,128)} copy(f32[1,32,512]{2,1,0:T(8,128)S(1)} %shard_map.73) | data formatting | bytes 131072
